TPU v7x, 32 devices: a whole 2x2x4 slice. The times are simulated.
32 devices in a mesh: dp: 8 (over y, x, core), tensor: 4 (over z).
Axes of the slice: x: 2, y: 2, z: 4, core: 2. Of those that a mesh axis runs over, the one named last changes fastest.
Arguments:
- tokens: bfloat16 [16384, 1024], P(('dp', 'tensor')), may hold values from -6 to 6
- cotangent: bfloat16 [16384, 1024], P(('dp', 'tensor')), may hold values from -6 to 6
- lengths: int32 [8, 3], P('dp'), may hold values from 1 to 1024, 1920 in all within a row
- token_order: int32 [16384], P(('dp', 'tensor')), may hold values from 0 to 16383, as said below
- token_return: int32 [16384], P(('dp', 'tensor')), may hold values from 0 to 16383, as said below
- w_mix: float32 [1024, 8, 768], P('dp', 'tensor'), may hold values from -0.1875 to 0.1875
- w_ba: float32 [1024, 8, 2], P('dp', 'tensor'), may hold values from -0.1875 to 0.1875
- conv_w: float32 [512, 8, 4], P('dp', 'tensor'), may hold values from -3 to 3
- w_out: float32 [1024, 8, 256], P('dp', 'tensor'), may hold values from -0.1875 to 0.1875
- w_gate_up: float32 [1024, 2, 2816], P('dp', None, 'tensor'), may hold values from -0.1875 to 0.1875
- w_down: float32 [1024, 2816], P('dp', 'tensor'), may hold values from -0.15625 to 0.15625
- gain_attn: float32 [1024], replicated, may hold values from 0.25 to 1.75
- gain_ffn: float32 [1024], replicated, may hold values from 0.25 to 1.75
- gain_out: float32 [256], replicated, may hold values from 0.25 to 1.75
- decay_log: float32 [8], replicated, may hold values from -8 to -3.5
- decay_bias: float32 [8], replicated, may hold values from -1 to 1
Outputs:
- layer_out: bfloat16 [16384, 1024], P(('dp', 'tensor'))
- input_grad: bfloat16 [16384, 1024], P(('dp', 'tensor'))
- grad_w_mix: float32 [1024, 8, 768], P('dp', 'tensor')
- grad_w_ba: float32 [1024, 8, 2], P('dp', 'tensor')
- grad_conv_w: float32 [512, 8, 4], P('dp', 'tensor')
- grad_w_out: float32 [1024, 8, 256], P('dp', 'tensor')
- grad_w_gate_up: float32 [1024, 2, 2816], P('dp', None, 'tensor')
- grad_w_down: float32 [1024, 2816], P('dp', 'tensor')
- grad_gain_attn: float32 [1024], replicated
- grad_gain_ffn: float32 [1024], replicated
- grad_gain_out: float32 [256], replicated
- grad_decay_log: float32 [8], replicated
- grad_decay_bias: float32 [8], replicated
Inputs may be any that keep to these rules, and one draw needn't show every extreme that they name: `lengths`: each row sums to 1920, and its largest entry is 1024. `token_order`: a permutation. Writing a row as 2048 * g + 512 * s + i with 0 <= i < 512, packed row and given row have the same s, and for every g and g' exactly 64 packed rows of group g' with a given s take given rows of group g. `token_return`: the inverse permutation of token_order.
All inputs are finite; a program needn't handle non-finite values.
Results may differ from a plain program's by a relative error of at most 0.015.
The roundings to bfloat16 on the way count: a program that leaves them out, or rounds other values in their place, can miss the bound.
Values may be sent and summed in bfloat16 or wider, within the bound.
No kernel may reach another device: no remote copies, remote signals or barrier semaphores. Data moves between devices by JAX's collectives and lax.ppermute only.
A program may use at most 256 MiB of HBM per device.

v0:
```python
import jax
import jax.numpy as jnp
from jax import lax
from jax.sharding import PartitionSpec as P

DK = 128
DV = 256
SPAN = 64
SEQS = 3
highest_precision = lax.Precision.HIGHEST
epsilon = 1e-06


def rms_scale(values):
    return lax.rsqrt(jnp.mean(values * values, axis=-1, keepdims=True) + epsilon)


def norm_rows(values, gain):
    return values * rms_scale(values) * gain


def segments(length_row, group_rows):
    seq_ends = jnp.cumsum(length_row)
    positions = jnp.arange(group_rows, dtype=jnp.int32)
    return jnp.sum((positions[:, None] >= seq_ends[None, :]).astype(jnp.int32), axis=1)


def short_conv(inputs, weights, segment_ids):
    row_count = inputs.shape[0]
    running = inputs * jnp.transpose(weights[:, :, 0])[None]
    for offset in range(1, weights.shape[2]):
        shifted = jnp.concatenate(
            [jnp.zeros((offset,) + inputs.shape[1:], inputs.dtype), inputs[: row_count - offset]],
            axis=0,
        )
        earlier = jnp.concatenate(
            [jnp.full((offset,), -1, jnp.int32), segment_ids[: row_count - offset]]
        )
        running = (
            running
            + jnp.where((earlier == segment_ids)[:, None, None], shifted, 0.0)
            * jnp.transpose(weights[:, :, offset])[None]
        )
    return running


def mixer_core(
    projected, small_proj, conv_weights, decay_rate, decay_shift, gain_norm, segment_ids, recurrence
):
    conv_width = 2 * DK + DV
    active = jax.nn.silu(short_conv(projected[:, :, :conv_width], conv_weights, segment_ids))
    query_vec = active[:, :, :DK]
    key_vec = active[:, :, DK : 2 * DK]
    value_vec = active[:, :, 2 * DK :]
    query_vec = (
        query_vec
        * lax.rsqrt(jnp.sum(query_vec * query_vec, axis=-1, keepdims=True) + epsilon)
        * DK ** (-0.5)
    )
    key_vec = key_vec * lax.rsqrt(jnp.sum(key_vec * key_vec, axis=-1, keepdims=True) + epsilon)
    beta_gate = jax.nn.sigmoid(small_proj[:, :, 0])
    log_decay = -jnp.exp(decay_rate)[None, :] * jax.nn.softplus(
        small_proj[:, :, 1] + decay_shift[None, :]
    )
    result = recurrence(query_vec, key_vec, value_vec, beta_gate, log_decay, segment_ids)
    normed = result * rms_scale(result) * gain_norm
    gated_out = normed * jax.nn.silu(projected[:, :, conv_width:])
    return gated_out * (segment_ids < SEQS).astype(gated_out.dtype)[:, None, None]


def delta_blocks(query_vec, key_vec, value_vec, beta_gate, log_decay, segment_ids):
    total_rows = query_vec.shape[0]
    block_count = total_rows // SPAN
    before_ids = jnp.concatenate([jnp.full((1,), -1, jnp.int32), segment_ids[:-1]])[::SPAN]
    lower_tri = jnp.tril(jnp.ones((SPAN, SPAN), dtype=bool))
    strict_tri = jnp.tril(jnp.ones((SPAN, SPAN), dtype=bool), -1)

    def split_rows(array):
        return array.reshape((block_count, SPAN) + array.shape[1:])

    def one_block(recurrent_matrix, pieces):
        query_rows, block_of_keys, values_block, beta_rows, decays, seg_block, before_id = pieces
        cumulative = jnp.cumsum(decays, axis=0)
        same_seg = seg_block[:, None] == seg_block[None, :]
        log_gap = cumulative[:, None, :] - cumulative[None, :, :]
        pairwise_decay = jnp.where(
            (same_seg & lower_tri)[:, :, None], jnp.exp(jnp.minimum(log_gap, 0.0)), 0.0
        )
        pairwise_decay = jnp.transpose(pairwise_decay, (2, 0, 1))
        carry_scale = jnp.transpose(
            jnp.where((seg_block == before_id)[:, None], jnp.exp(cumulative), 0.0)
        )
        beta_cols = jnp.transpose(beta_rows)[:, :, None]
        key_key = jnp.einsum(
            "ihk,jhk->hij", block_of_keys, block_of_keys, precision=highest_precision
        )
        lower_part = jnp.where(strict_tri[None], pairwise_decay * key_key, 0.0) * beta_cols
        key_state_product = jnp.einsum(
            "grm,rmj->rgj", block_of_keys, recurrent_matrix, precision=highest_precision
        )
        right_side = beta_cols * (
            jnp.transpose(values_block, (1, 0, 2)) - carry_scale[:, :, None] * key_state_product
        )
        delta_update_rows = jax.scipy.linalg.solve_triangular(
            lower_part, right_side, lower=True, unit_diagonal=True
        )
        query_state_product = jnp.einsum(
            "grm,rmj->rgj", query_rows, recurrent_matrix, precision=highest_precision
        )
        query_key = jnp.einsum(
            "ihk,jhk->hij", query_rows, block_of_keys, precision=highest_precision
        )
        outputs = carry_scale[:, :, None] * query_state_product + jnp.einsum(
            "hij,hjv->hiv",
            query_key * pairwise_decay,
            delta_update_rows,
            precision=highest_precision,
        )
        new_state = carry_scale[:, -1][:, None, None] * recurrent_matrix + jnp.einsum(
            "tdx,dt,dtg->dxg",
            block_of_keys,
            pairwise_decay[:, -1, :],
            delta_update_rows,
            precision=highest_precision,
        )
        return (new_state, jnp.transpose(outputs, (1, 0, 2)))

    block_items = (
        split_rows(query_vec),
        split_rows(key_vec),
        split_rows(value_vec),
        split_rows(beta_gate),
        split_rows(log_decay),
        split_rows(segment_ids),
        before_ids,
    )
    initial = jnp.zeros((query_vec.shape[1], DK, DV), query_vec.dtype)
    outputs = lax.scan(jax.checkpoint(one_block), initial, block_items)[1]
    return outputs.reshape(total_rows, query_vec.shape[1], DV)


def body(
    tokens,
    cotangent,
    lengths,
    token_order,
    token_return,
    w_mix,
    w_ba,
    conv_w,
    w_out,
    w_gate_up,
    w_down,
    gain_attn,
    gain_ffn,
    gain_out,
    decay_log,
    decay_bias,
):
    groups = lax.axis_size("dp")
    splits = lax.axis_size("tensor")
    local_rows = tokens.shape[0]
    model_width = tokens.shape[1]
    group_rows = local_rows * splits
    per_peer = local_rows // groups
    send_key = token_return // group_rows * local_rows + token_return % local_rows
    send_order = jnp.argsort(send_key)
    recv_key = token_order // group_rows * local_rows + jnp.arange(local_rows, dtype=jnp.int32)
    recv_order = jnp.argsort(recv_key)
    recv_place = jnp.argsort(recv_order)
    arrived = (
        lax.all_to_all(
            tokens[send_order].reshape(groups, per_peer, model_width),
            "dp",
            split_axis=0,
            concat_axis=0,
            tiled=True,
        ),
        lax.all_to_all(
            cotangent[send_order].reshape(groups, per_peer, model_width),
            "dp",
            split_axis=0,
            concat_axis=0,
            tiled=True,
        ),
    )
    packed_in = arrived[0].reshape(local_rows, model_width)[recv_place]
    packed_grad = arrived[1].reshape(local_rows, model_width)[recv_place]
    segment_ids = segments(lengths[0], group_rows)
    row_mask = (segment_ids < SEQS).astype(jnp.float32)[:, None]
    mix_all, small_all, conv_all, out_all, ffn_all, down_all = (
        lax.all_gather(w_mix.astype(jnp.bfloat16), "dp", axis=0, tiled=True),
        lax.all_gather(w_ba.astype(jnp.bfloat16), "dp", axis=0, tiled=True),
        lax.all_gather(conv_w.astype(jnp.bfloat16), "dp", axis=0, tiled=True),
        lax.all_gather(w_out.astype(jnp.bfloat16), "dp", axis=0, tiled=True),
        lax.all_gather(w_gate_up.astype(jnp.bfloat16), "dp", axis=0, tiled=True),
        lax.all_gather(w_down.astype(jnp.bfloat16), "dp", axis=0, tiled=True),
    )
    input_f32 = packed_in.astype(jnp.float32)
    normed_f32, norm_attn_back = jax.vjp(norm_rows, input_f32, gain_attn)
    normed_all, grad_all = (
        lax.all_gather(normed_f32.astype(jnp.bfloat16), "tensor", axis=0, tiled=True),
        lax.all_gather(packed_grad, "tensor", axis=0, tiled=True),
    )
    projected = jnp.einsum("td,dhp->thp", normed_all, mix_all, preferred_element_type=jnp.float32)
    small_proj = jnp.einsum(
        "td,dhc->thc", normed_all, small_all, preferred_element_type=jnp.float32
    )
    heads_here = mix_all.shape[1]
    head_start = lax.axis_index("tensor") * heads_here
    rate_here = lax.dynamic_slice_in_dim(decay_log, head_start, heads_here)
    shift_here = lax.dynamic_slice_in_dim(decay_bias, head_start, heads_here)

    def core_pass(proj_in, small_in, conv_in, rate_in, shift_in, gain_in):
        return mixer_core(
            proj_in, small_in, conv_in, rate_in, shift_in, gain_in, segment_ids, delta_blocks
        )

    gated_f32, core_back = jax.vjp(
        core_pass,
        projected,
        small_proj,
        conv_all.astype(jnp.float32),
        rate_here,
        shift_here,
        gain_out,
    )
    gated_out = gated_f32.astype(jnp.bfloat16)
    middle = input_f32 + lax.psum_scatter(
        jnp.einsum("thv,dhv->td", gated_out, out_all, preferred_element_type=jnp.float32),
        "tensor",
        scatter_dimension=0,
        tiled=True,
    )
    normed_mid_f32, norm_ffn_back = jax.vjp(norm_rows, middle, gain_ffn)
    normed_mid_all = lax.all_gather(
        normed_mid_f32.astype(jnp.bfloat16), "tensor", axis=0, tiled=True
    )
    gate_up = jnp.einsum("td,dcf->tcf", normed_mid_all, ffn_all, preferred_element_type=jnp.float32)

    def activate(pair_in):
        return jax.nn.silu(pair_in[:, 0]) * pair_in[:, 1] * row_mask

    hidden_f32, act_back = jax.vjp(activate, gate_up)
    hidden = hidden_f32.astype(jnp.bfloat16)
    layer_rows = (
        middle
        + lax.psum_scatter(
            jnp.einsum("tf,df->td", hidden, down_all, preferred_element_type=jnp.float32).astype(
                jnp.bfloat16
            ),
            "tensor",
            scatter_dimension=0,
            tiled=True,
        ).astype(jnp.float32)
    ).astype(jnp.bfloat16)
    grad_down = jnp.einsum("td,tf->df", grad_all, hidden, preferred_element_type=jnp.float32)
    grad_hidden = jnp.einsum("td,df->tf", grad_all, down_all, preferred_element_type=jnp.float32)
    grad_pair = act_back(grad_hidden)[0].astype(jnp.bfloat16)
    grad_ffn_w = jnp.einsum(
        "td,tcf->dcf", normed_mid_all, grad_pair, preferred_element_type=jnp.float32
    )
    grad_mid_norm, grad_gain_ffn = norm_ffn_back(
        lax.psum_scatter(
            jnp.einsum("tcf,dcf->td", grad_pair, ffn_all, preferred_element_type=jnp.float32),
            "tensor",
            scatter_dimension=0,
            tiled=True,
        )
    )
    grad_middle = packed_grad.astype(jnp.float32) + grad_mid_norm
    grad_middle_all = lax.all_gather(grad_middle.astype(jnp.bfloat16), "tensor", axis=0, tiled=True)
    grad_out_w = jnp.einsum(
        "thv,td->dhv", gated_out, grad_middle_all, preferred_element_type=jnp.float32
    )
    grad_gated = jnp.einsum(
        "td,dhv->thv", grad_middle_all, out_all, preferred_element_type=jnp.float32
    )
    grad_proj, grad_small, grad_conv, grad_rate, grad_shift, grad_gain_out = core_back(grad_gated)
    grad_proj = grad_proj.astype(jnp.bfloat16)
    grad_small = grad_small.astype(jnp.bfloat16)
    grad_mix_w = jnp.einsum(
        "td,thp->dhp", normed_all, grad_proj, preferred_element_type=jnp.float32
    )
    grad_small_w = jnp.einsum(
        "td,thc->dhc", normed_all, grad_small, preferred_element_type=jnp.float32
    )
    grad_normed = lax.psum_scatter(
        (
            jnp.einsum("thp,dhp->td", grad_proj, mix_all, preferred_element_type=jnp.float32)
            + jnp.einsum("thc,dhc->td", grad_small, small_all, preferred_element_type=jnp.float32)
        ).astype(jnp.bfloat16),
        "tensor",
        scatter_dimension=0,
        tiled=True,
    ).astype(jnp.float32)
    grad_input_norm, grad_gain_attn = norm_attn_back(grad_normed)
    grad_rows = (grad_middle + grad_input_norm).astype(jnp.bfloat16)
    owned = (
        lax.psum_scatter(grad_mix_w, "dp", scatter_dimension=0, tiled=True),
        lax.psum_scatter(grad_small_w, "dp", scatter_dimension=0, tiled=True),
        lax.psum_scatter(grad_conv, "dp", scatter_dimension=0, tiled=True),
        lax.psum_scatter(grad_out_w, "dp", scatter_dimension=0, tiled=True),
        lax.psum_scatter(grad_ffn_w, "dp", scatter_dimension=0, tiled=True),
        lax.psum_scatter(grad_down, "dp", scatter_dimension=0, tiled=True),
    )
    head_total = decay_log.shape[0]
    rate_full = lax.dynamic_update_slice_in_dim(
        jnp.zeros((head_total,), jnp.float32), grad_rate, head_start, 0
    )
    shift_full = lax.dynamic_update_slice_in_dim(
        jnp.zeros((head_total,), jnp.float32), grad_shift, head_start, 0
    )
    small_sums = lax.psum(
        (grad_gain_attn, grad_gain_ffn, grad_gain_out, rate_full, shift_full), ("dp", "tensor")
    )
    returned = (
        lax.all_to_all(
            layer_rows[recv_order].reshape(groups, per_peer, model_width),
            "dp",
            split_axis=0,
            concat_axis=0,
            tiled=True,
        ),
        lax.all_to_all(
            grad_rows[recv_order].reshape(groups, per_peer, model_width),
            "dp",
            split_axis=0,
            concat_axis=0,
            tiled=True,
        ),
    )
    back_place = jnp.argsort(send_order)
    layer_out = returned[0].reshape(local_rows, model_width)[back_place]
    input_grad = returned[1].reshape(local_rows, model_width)[back_place]
    return (
        layer_out,
        input_grad,
        owned[0],
        owned[1],
        owned[2],
        owned[3],
        owned[4],
        owned[5],
        small_sums[0],
        small_sums[1],
        small_sums[2],
        small_sums[3],
        small_sums[4],
    )


def solution(mesh):
    placed = (
        P(("dp", "tensor"), None),
        P(("dp", "tensor"), None),
        P("dp", None),
        P(("dp", "tensor")),
        P(("dp", "tensor")),
        P("dp", "tensor", None),
        P("dp", "tensor", None),
        P("dp", "tensor", None),
        P("dp", "tensor", None),
        P("dp", None, "tensor"),
        P("dp", "tensor"),
        P(),
        P(),
        P(),
        P(),
        P(),
    )
    return jax.shard_map(
        body,
        mesh=mesh,
        in_specs=placed,
        out_specs=(
            P(("dp", "tensor"), None),
            P(("dp", "tensor"), None),
            P("dp", "tensor", None),
            P("dp", "tensor", None),
            P("dp", "tensor", None),
            P("dp", "tensor", None),
            P("dp", None, "tensor"),
            P("dp", "tensor"),
            P(),
            P(),
            P(),
            P(),
            P(),
        ),
        check_vma=False,
    )
```

profile of v0, /device:TPU:0, one launch (start us, length us, event | category | flops | bytes accessed | tf_op | source)
XLA Modules:
  0.0 3141.6 jit_solution(17922218729090918797)
XLA Ops:
  30.0 9.9 all-to-all-done
  68.7 65.3 %all-gather.10.cloned.1.call-done = bf16[2048,1024]{1,0:T(8,128)(2,1)} async-done(((bf16[512,1024]{1,0:T(8,128)(2,1)}), bf16[2048,1024]{1,0:T(8,128)(2,1)}) %all-gather.10.cloned.1.call-update) | async-done | bytes 4194320 | tf_op jit(solution)/shard_map/all_gather | solution.py:202
  157.5 14.5 fusion.136
  192.0 641.0 %while.41 = (s32[]{:T(128)}, f32[2,128,256]{2,1,0:T(8,128)S(1)}, f32[32,64,2,256]{3,1,2,0:T(8,128)}, f32[32,2,128,256]{3,2,1,0:T(8,128)}, s32[32,64]{1,0:T(8,128...) while((s32[]{:T(128)}, f32[2,128,256]{2,1,0:T(8,128)S(1)}, ...), condition=%wide.region_10.12_spmd.clone, body=%wide.region_8.11_spmd.clone.sunk | while | flops 227238144 | bytes 3428001 | solution.py:138
  256.4 9.8 custom-call.42
  316.5 9.8 custom-call.42
  536.8 9.8 custom-call.42
  853.2 141.1 %reduce-scatter.15.cloned.1.call-done = f32[512,1024]{1,0:T(8,128)} async-done(((f32[2048,1024]{1,0:T(8,128)}), f32[512,1024]{1,0:T(8,128)}) %reduce-scatter.15.cloned.1.call-update) | async-done | bytes 2097168 | tf_op jit(solution)/shard_map/reduce_scatter | solution.py:229
  1002.0 21.4 all_to_all.20
  1026.2 10.4 all-gather.18.cloned.1.call-done
  1036.6 82.8 %all-gather.16.cloned.1.call-done = bf16[2048,1024]{1,0:T(8,128)(2,1)} async-done(((bf16[512,1024]{1,0:T(8,128)(2,1)}), bf16[2048,1024]{1,0:T(8,128)(2,1)}) %all-gather.16.cloned.1.call-update) | async-done | bytes 4194320 | tf_op jit(solution)/shard_map/all_gather | solution.py:236
  1119.4 12.0 fusion.149
  1131.5 14.3 all-gather.20.cloned.1.call-done
  1145.7 82.4 %all-gather.24.cloned.1.call-done = bf16[2048,1024]{1,0:T(8,128)(2,1)} async-done(((bf16[512,1024]{1,0:T(8,128)(2,1)}), bf16[2048,1024]{1,0:T(8,128)(2,1)}) %all-gather.24.cloned.1.call-update) | async-done | bytes 4194320 | tf_op jit(solution)/shard_map/all_gather | solution.py:203
  1228.1 11.4 multiply_bitcast_fusion
  1253.0 143.1 %reduce-scatter.19.cloned.1.call-done = f32[512,1024]{1,0:T(8,128)} async-done(((f32[2048,1024]{1,0:T(8,128)}), f32[512,1024]{1,0:T(8,128)}) %reduce-scatter.19.cloned.1.call-update) | async-done | bytes 2097168 | tf_op jit(solution)/shard_map/reduce_scatter | solution.py:264
  1402.6 79.7 %all-gather.22.cloned.1.call-done = bf16[2048,1024]{1,0:T(8,128)(2,1)} async-done(((bf16[512,1024]{1,0:T(8,128)(2,1)}), bf16[2048,1024]{1,0:T(8,128)(2,1)}) %all-gather.22.cloned.1.call-update) | async-done | bytes 4194320 | tf_op jit(solution)/shard_map/all_gather | solution.py:272
  1482.3 10.6 multiply_reduce_fusion.9
  1502.3 1108.9 %while.42 = (s32[]{:T(128)}, f32[2,128,256]{2,1,0:T(8,128)}, f32[32,64,2,128]{3,1,0,2:T(8,128)}, f32[32,64,2,128]{3,1,0,2:T(8,128)S(1)}, f32[32,64,2,256]{3,1,0,...) while((s32[]{:T(128)}, f32[2,128,256]{2,1,0:T(8,128)}, ...), condition=%wide.region_29.31_spmd.clone, body=%wide.region_19.30_spmd.clone.sunk | while | flops 612151424 | bytes 10787363 | solution.py:138
  2625.6 16.1 multiply_reduce_fusion.8
  2653.5 13.7 multiply_add_fusion
  2700.7 12.9 fusion.152
  2721.7 11.8 fusion.147
  2734.2 21.6 reduce-scatter.21.cloned.1.call-done
  2758.0 77.4 %reduce-scatter.17.cloned.1.call-done = bf16[512,1024]{1,0:T(8,128)(2,1)} async-done(((bf16[2048,1024]{1,0:T(8,128)(2,1)}), bf16[512,1024]{1,0:T(8,128)(2,1)}) %reduce-scatter.17.cloned.1.call-update) | async-done | bytes 1048592 | tf_op jit(solution)/shard_map/reduce_scatter | solution.py:248
  2848.5 12.6 all-to-all-done.3
  2875.0 37.1 %reduce-scatter.31.cloned.1.call-done = f32[128,4]{1,0:T(8,128)} async-done(((f32[1024,4]{1,0:T(8,128)}), f32[128,4]{1,0:T(8,128)}) %reduce-scatter.31.cloned.1.call-update) | async-done | bytes 2064
  2913.6 42.9 %reduce-scatter.25.cloned.1.call-done = f32[128,2,256]{2,0,1:T(8,128)} async-done(((f32[1024,2,256]{2,0,1:T(8,128)}), f32[128,2,256]{2,0,1:T(8,128)}) %reduce-scatter.25.cloned.1.call-update) | async-done | bytes 262160 | tf_op jit(solution)/shard_map/reduce_scatter | solution.py:303
  2958.3 39.9 %all-reduce.23 = (f32[1024]{0:T(1024)}, f32[1024]{0:T(1024)}, f32[256]{0:T(256)}, f32[8]{0:T(128)}, f32[8]{0:T(128)}) all-reduce(f32[1024]{0:T(1024)S(1)} %get-tuple-element.900, f32[1024]{0:T(1024)S(1)} %copy-done.65, f32[256]{0:T(256)S(1)} %copy-done.85, ...), channel_id=1, replica_groups=mesh['dp'=8,'tensor'=4] {'dp','tensor'}, use_global_device_ids=true, to_apply=%region_45.47 | all-reduce | flops 2320 | bytes 18560 | tf_op jit(solution)/shard_map/psum | solution.py:314
  3003.8 18.7 reduce-scatter.23.cloned.1.call-done
  3025.1 46.1 %reduce-scatter.29.cloned.1.call-done = f32[128,704]{0,1:T(8,128)} async-done(((f32[1024,704]{0,1:T(8,128)}), f32[128,704]{0,1:T(8,128)}) %reduce-scatter.29.cloned.1.call-update) | async-done | bytes 360464 | tf_op jit(solution)/shard_map/reduce_scatter | solution.py:305
  3071.2 63.3 %reduce-scatter.27.cloned.1.call-done = f32[128,2,704]{0,2,1:T(8,128)} async-done(((f32[1024,2,704]{0,2,1:T(8,128)}), f32[128,2,704]{0,2,1:T(8,128)}) %reduce-scatter.27.cloned.1.call-update) | async-done | bytes 720912 | tf_op jit(solution)/shard_map/reduce_scatter | solution.py:304
  (2959 shorter events, 1974.3 us)
Async XLA Ops:
  7.2 61.5 %all-gather.12.cloned.1.call-start = ((), (), s32[]{:S(2)}) async-start(), calls=%async_computation.15 | async-start | bytes 3538944 | tf_op jit(solution)/shard_map/all_gather | solution.py:192
  17.1 22.7 all-to-all-start
  22.3 111.7 %all-gather.10.cloned.1.call-start = ((), (), s32[]{:S(2)}) async-start(), calls=%async_computation.14 | async-start | bytes 5242880 | tf_op jit(solution)/shard_map/all_gather | solution.py:202
  43.6 800.0 %all-gather.14.cloned.1.call-start = ((), (), s32[]{:S(2)}) async-start(), calls=%async_computation.16 | async-start | bytes 1179648 | tf_op jit(solution)/shard_map/all_gather | solution.py:195
  44.4 949.9 %reduce-scatter.15.cloned.1.call-start = ((), (), s32[]{:S(2)}) async-start(), calls=%async_computation.17 | async-start | bytes 10485760 | tf_op jit(solution)/shard_map/reduce_scatter | solution.py:229
  68.6 770.7 %copy-start.55 = (f32[2048]{0:T(1024)}, f32[2048]{0:T(1024)S(1)}, u32[]{:S(2)}) copy-start(f32[2048]{0:T(1024)S(1)} %get-tuple-element.1014) | copy-start | bytes 24580
  68.6 1332.0 %copy-start.48 = (pred[2048]{0:T(1024)(128)(4,1)}, pred[2048]{0:T(1024)(128)(4,1)S(1)}, u32[]{:S(2)}) copy-start(pred[2048]{0:T(1024)(128)(4,1)S(1)} %get-tuple-element.1015) | copy-start | bytes 6148
  68.6 1332.7 %copy-start.50 = (pred[2048]{0:T(1024)(128)(4,1)}, pred[2048]{0:T(1024)(128)(4,1)S(1)}, u32[]{:S(2)}) copy-start(pred[2048]{0:T(1024)(128)(4,1)S(1)} %get-tuple-element.1016) | copy-start | bytes 6148
  851.2 145.8 %copy-start.32 = (f32[1024]{0:T(1024)S(1)}, f32[1024]{0:T(1024)}, u32[]{:S(2)}) copy-start(f32[1024]{0:T(1024)} %param.34) | copy-start | bytes 12292
  851.2 185.4 %all-gather.18.cloned.1.call-start = ((), (), s32[]{:S(2)}) async-start(), calls=%async_computation.19 | async-start | bytes 3244032 | tf_op jit(solution)/shard_map/all_gather | solution.py:196
  853.1 145.2 %copy-start.21 = (f32[128,704]{0,1:T(8,128)S(1)}, f32[128,704]{0,1:T(8,128)}, u32[]{:S(2)}) copy-start(f32[128,704]{0,1:T(8,128)} %param.32) | copy-start | bytes 1081348
  853.1 146.0 %copy-start.4 = (bf16[512,1024]{1,0:T(8,128)(2,1)S(1)}, bf16[512,1024]{1,0:T(8,128)(2,1)}, u32[]{:S(2)}) copy-start(bf16[512,1024]{1,0:T(8,128)(2,1)} %param.23) | copy-start | bytes 3145732
  853.1 266.3 %all-gather.16.cloned.1.call-start = ((), (), s32[]{:S(2)}) async-start(), calls=%async_computation.18 | async-start | bytes 5242880 | tf_op jit(solution)/shard_map/all_gather | solution.py:236
  996.4 402.5 %copy-start.5 = (f32[512,1024]{1,0:T(8,128)}, f32[512,1024]{1,0:T(8,128)S(1)}, u32[]{:S(2)}) copy-start(f32[512,1024]{1,0:T(8,128)S(1)} %get-tuple-element.970) | copy-start | bytes 6291460
  997.0 401.9 %copy-start.35 = (f32[512]{0:T(512)}, f32[512]{0:T(512)S(1)}, u32[]{:S(2)}) copy-start(f32[512]{0:T(512)S(1)} %fusion.195) | copy-start | bytes 6148
  998.2 147.5 %all-gather.20.cloned.1.call-start = ((), (), s32[]{:S(2)}) async-start(), calls=%async_computation.20 | async-start | bytes 1622016 | tf_op jit(solution)/shard_map/all_gather | solution.py:197
  999.0 229.1 %all-gather.24.cloned.1.call-start = ((), (), s32[]{:S(2)}) async-start(), calls=%async_computation.29 | async-start | bytes 5242880 | tf_op jit(solution)/shard_map/all_gather | solution.py:203
  1026.2 201.9 %copy-start.56 = (f32[2048]{0:T(1024)S(1)}, f32[2048]{0:T(1024)}, u32[]{:S(2)}) copy-start(f32[2048]{0:T(1024)} %copy-done.55) | copy-start | bytes 24580
  1026.2 369.8 %reduce-scatter.19.cloned.1.call-start = ((), (), s32[]{:S(2)}) async-start(), calls=%async_computation.22 | async-start | bytes 10485760 | tf_op jit(solution)/shard_map/reduce_scatter | solution.py:264
  1252.9 146.0 %copy-start.64 = (f32[512]{0:T(512)S(1)}, f32[512]{0:T(512)}, u32[]{:S(2)}) copy-start(f32[512]{0:T(512)} %copy-done.63) | copy-start | bytes 6148
  1252.9 146.0 %copy-start.11 = (bf16[512,1024]{1,0:T(8,128)(2,1)S(1)}, bf16[512,1024]{1,0:T(8,128)(2,1)}, u32[]{:S(2)}) copy-start(bf16[512,1024]{1,0:T(8,128)(2,1)} %gather_fusion.5) | copy-start | bytes 3145732
  1252.9 229.4 %all-gather.22.cloned.1.call-start = ((), (), s32[]{:S(2)}) async-start(), calls=%async_computation.23 | async-start | bytes 5242880 | tf_op jit(solution)/shard_map/all_gather | solution.py:272
  1400.6 1355.2 %reduce-scatter.21.cloned.1.call-start = ((), (), s32[]{:S(2)}) async-start(), calls=%async_computation.24 | async-start | bytes 5242880 | tf_op jit(solution)/shard_map/reduce_scatter | solution.py:288
  2680.3 155.0 %reduce-scatter.17.cloned.1.call-start = ((), (), s32[]{:S(2)}) async-start(), calls=%async_computation.21 | async-start | bytes 5242880 | tf_op jit(solution)/shard_map/reduce_scatter | solution.py:248
  2688.6 184.8 %reduce-scatter.33.cloned.1.call-start = ((), (), s32[]{:S(2)}) async-start(), calls=%async_computation.31 | async-start | bytes 294912
  2690.3 221.8 %reduce-scatter.31.cloned.1.call-start = ((), (), s32[]{:S(2)}) async-start(), calls=%async_computation.30 | async-start | bytes 589824
  2694.7 261.8 %reduce-scatter.25.cloned.1.call-start = ((), (), s32[]{:S(2)}) async-start(), calls=%async_computation.26 | async-start | bytes 2359296 | tf_op jit(solution)/shard_map/reduce_scatter | solution.py:303
  2700.6 321.9 %reduce-scatter.23.cloned.1.call-start = ((), (), s32[]{:S(2)}) async-start(), calls=%async_computation.25 | async-start | bytes 7077888 | tf_op jit(solution)/shard_map/reduce_scatter | solution.py:300
  2713.6 357.6 %reduce-scatter.29.cloned.1.call-start = ((), (), s32[]{:S(2)}) async-start(), calls=%async_computation.28 | async-start | bytes 3244032 | tf_op jit(solution)/shard_map/reduce_scatter | solution.py:305
  2721.5 413.0 %reduce-scatter.27.cloned.1.call-start = ((), (), s32[]{:S(2)}) async-start(), calls=%async_computation.27 | async-start | bytes 6488064 | tf_op jit(solution)/shard_map/reduce_scatter | solution.py:304
  2842.0 19.1 all-to-all-start.3
  2861.1 140.0 %all-to-all-start.1 = ((bf16[8,64,1024]{2,1,0:T(8,128)(2,1)}), bf16[8,64,1024]{2,1,0:T(8,128)(2,1)S(1)}, u32[]{:S(2)}, u32[]{:S(2)}) async-start(bf16[8,64,1024]{2,1,0:T(8,128)(2,1)} %bitcast.548), calls=%async_computation.3 | async-start | bytes 2097152 | tf_op jit(solution)/shard_map/all_to_all | solution.py:318
  (117 other events, 2354.4 us)
Sparse Core Ops, SparseCore 0:
  10.5 40.4 all-gather.11
  53.2 80.7 all-gather.9
  136.5 22.0 all-gather.13
  851.3 142.8 reduce-scatter.14
  996.5 40.0 all-gather.17
  1038.6 80.7 all-gather.15
  1121.9 23.8 all-gather.19
  1147.3 80.7 all-gather.23
  1253.0 142.9 reduce-scatter.18
  1400.7 81.5 all-gather.21
  2680.5 75.2 reduce-scatter.20
  2758.0 77.2 reduce-scatter.16
  2838.9 34.4 reduce-scatter.32
  2877.2 34.8 reduce-scatter.30
  2915.2 41.1 reduce-scatter.24
  2960.1 62.3 reduce-scatter.22
  3026.3 44.8 reduce-scatter.28
  3075.4 59.0 reduce-scatter.26
where the time goes:
time: 3170 us; the launch traced here: 3140 us
  other arithmetic  978 us (31%)
  waiting for transfers between devices  951 us (30%)
  matrix products  627 us (20%)
  local copies, waits for them, and re-layouts  469 us (15%)
  blocking collectives  78.5 us (2%)
    another operation x256, other arithmetic, one_block(): jax.scipy.linalg.solve_triangular(lower_part, right_side, lower=True, uni...  638 us
    squeeze x256, local copies, waits for them, and re-layouts, delta_blocks(): outputs = lax.scan(jax.checkpoint(one_block), initial, block_items)[1]  187 us
    reduce_scatter x1, waiting for transfers between devices, body(): lax.psum_scatter(jnp.einsum('tcf,dcf->td', grad_pair, ffn_all, preferred_...  143 us
    reduce_scatter x1, waiting for transfers between devices, body(): lax.psum_scatter(jnp.einsum('thv,dhv->td', gated_out, out_all, preferred_...  141 us
    dot_general x128, matrix products, one_block(): jnp.einsum('ihk,jhk->hij', query_rows, block_of_keys, precision=highest_p...  109 us
    dot_general x128, matrix products, one_block(): jnp.einsum('grm,rmj->rgj', block_of_keys, recurrent_matrix, precision=hig...  101 us
    dot_general x128, matrix products, one_block(): jnp.einsum('grm,rmj->rgj', query_rows, recurrent_matrix, precision=highes...  95.9 us
    all_gather x1, waiting for transfers between devices, body(): lax.all_gather(normed_mid_f32.astype(jnp.bfloat16), 'tensor', axis=0, til...  82.8 us
  transfers between devices with their start and end apart: 21, of which 18 were waited for; matrix products, arithmetic and copies ran while one was open for 27% of the time, Pallas kernels for 0%

commit v1 on v0

--- a/solution.py
+++ b/solution.py
@@ -9,6 +9,29 @@
 SEQS = 3
 highest_precision = lax.Precision.HIGHEST
 epsilon = 1e-06
+
+
+def settle_surface(row_data, array_axis):
+    row_data = jnp.moveaxis(row_data, 0, array_axis)
+    high = row_data.shape
+    block_last = row_data.reshape(
+        *high[:array_axis], high[array_axis] * high[array_axis + 1], *high[array_axis + 2 :]
+    )
+    return block_last
+
+
+def _proceed_digits(t0, device_axis):
+    chips = lax.axis_size(device_axis)
+    oldest = t0[None]
+    for ix in range(chips.bit_length() - 1):
+        big = 1 << ix
+        response = lax.ppermute(
+            oldest, device_axis, list(map(lambda u: (u, u ^ big), range(chips)))
+        )
+        small = jnp.stack([oldest, response], 0)
+        next_value = lax.axis_index(device_axis) >> ix & 1
+        oldest = jnp.where(next_value == 0, small, small[::-1]).reshape(-1, *t0.shape)
+    return oldest
 
 
 def rms_scale(values):
@@ -198,9 +221,14 @@
     )
     input_f32 = packed_in.astype(jnp.float32)
     normed_f32, norm_attn_back = jax.vjp(norm_rows, input_f32, gain_attn)
+
+    def expand_grid(matrix, q_in, axis_k=0):
+        after = settle_surface(_proceed_digits(matrix, q_in), axis_k)
+        return after
+
     normed_all, grad_all = (
         lax.all_gather(normed_f32.astype(jnp.bfloat16), "tensor", axis=0, tiled=True),
-        lax.all_gather(packed_grad, "tensor", axis=0, tiled=True),
+        expand_grid(packed_grad, "tensor"),
     )
     projected = jnp.einsum("td,dhp->thp", normed_all, mix_all, preferred_element_type=jnp.float32)
     small_proj = jnp.einsum(

time: 3170 us -> 3170 us (level)
    ppermute x0 -> x2, waiting for transfers between devices: none -> 174 us  [_proceed_digits(): lax.ppermute(oldest, device_axis, list(map(lambda u: (u, u ^ big), range(...]
    all_gather x1, waiting for transfers between devices: 82.8 us -> 0.01 us  [body(): lax.all_gather(normed_mid_f32.astype(jnp.bfloat16), 'tensor', axis=0, til...]
    all_gather x1 -> x0, waiting for transfers between devices: 82.4 us -> none  [body(): lax.all_gather(packed_grad, 'tensor', axis=0, tiled=True)]
  transfers between devices with their start and end apart: 21 -> 22, of which waited for: 18 -> 16; matrix products, arithmetic and copies ran while one was open for 27% -> 27% of each run, Pallas kernels for 0% -> 0%
where the time goes in v1:
time: 3170 us; the launch traced here: 3140 us
  other arithmetic  988 us (31%)
  waiting for transfers between devices  932 us (29%)
  matrix products  633 us (20%)
  local copies, waits for them, and re-layouts  468 us (15%)
  blocking collectives  79.7 us (3%)
    another operation x256, other arithmetic, one_block(): jax.scipy.linalg.solve_triangular(lower_part, right_side, lower=True, uni...  638 us
    squeeze x256, local copies, waits for them, and re-layouts, delta_blocks(): outputs = lax.scan(jax.checkpoint(one_block), initial, block_items)[1]  187 us
    ppermute x2, waiting for transfers between devices, _proceed_digits(): lax.ppermute(oldest, device_axis, list(map(lambda u: (u, u ^ big), range(...  174 us
    reduce_scatter x1, waiting for transfers between devices, body(): lax.psum_scatter(jnp.einsum('tcf,dcf->td', grad_pair, ffn_all, preferred_...  143 us
    reduce_scatter x1, waiting for transfers between devices, body(): lax.psum_scatter(jnp.einsum('thv,dhv->td', gated_out, out_all, preferred_...  141 us
    dot_general x128, matrix products, one_block(): jnp.einsum('ihk,jhk->hij', query_rows, block_of_keys, precision=highest_p...  110 us
    dot_general x128, matrix products, one_block(): jnp.einsum('grm,rmj->rgj', block_of_keys, recurrent_matrix, precision=hig...  101 us
    dot_general x128, matrix products, one_block(): jnp.einsum('grm,rmj->rgj', query_rows, recurrent_matrix, precision=highes...  95.8 us
  transfers between devices with their start and end apart: 22, of which 16 were waited for; matrix products, arithmetic and copies ran while one was open for 27% of the time, Pallas kernels for 0%

profile of v1, /device:TPU:0, one launch (start us, length us, event | category | flops | bytes accessed | tf_op | source)
XLA Modules:
  0.0 3143.6 jit_solution(2965207253680491424)
XLA Ops:
  29.4 10.5 all-to-all-done
  68.6 68.5 %all-gather.8.cloned.1.call-done = bf16[2048,1024]{1,0:T(8,128)(2,1)} async-done(((bf16[512,1024]{1,0:T(8,128)(2,1)}), bf16[2048,1024]{1,0:T(8,128)(2,1)}) %all-gather.8.cloned.1.call-update) | async-done | bytes 4194320 | tf_op jit(solution)/shard_map/all_gather | solution.py:230
  160.8 14.5 fusion.136
  195.3 641.2 %while.41 = (s32[]{:T(128)}, f32[2,128,256]{2,1,0:T(8,128)S(1)}, f32[32,64,2,256]{3,1,2,0:T(8,128)}, f32[32,2,128,256]{3,2,1,0:T(8,128)}, s32[32,64]{1,0:T(8,128...) while((s32[]{:T(128)}, f32[2,128,256]{2,1,0:T(8,128)S(1)}, ...), condition=%wide.region_10.12_spmd.clone, body=%wide.region_8.11_spmd.clone.sunk | while | flops 227238144 | bytes 3428001 | solution.py:161
  219.8 9.8 custom-call.42
  259.9 9.8 custom-call.42
  360.0 9.8 custom-call.42
  856.8 141.0 %reduce-scatter.15.cloned.1.call-done = f32[512,1024]{1,0:T(8,128)} async-done(((f32[2048,1024]{1,0:T(8,128)}), f32[512,1024]{1,0:T(8,128)}) %reduce-scatter.15.cloned.1.call-update) | async-done | bytes 2097168 | tf_op jit(solution)/shard_map/reduce_scatter | solution.py:257
  1004.4 22.6 all_to_all.20
  1031.2 23.7 collective-permute-done
  1062.5 150.0 %collective-permute-done.1 = bf16[2,512,1024]{2,1,0:T(8,128)(2,1)} collective-permute-done((bf16[2,512,1024]{2,1,0:T(8,128)(2,1)}, bf16[2,512,1024]{2,1,0:T(8,128)(2,1)}, u32[]{:S(2)}, u32[]{:S(2)}) %collective-permute-start.1) | collective-permute-done | bytes 2097184 | tf_op jit(solution)/shard_map/ppermute | solution.py:28
  1218.3 11.9 fusion.153
  1230.2 9.8 multiply_bitcast_fusion
  1253.4 143.4 %reduce-scatter.19.cloned.1.call-done = f32[512,1024]{1,0:T(8,128)} async-done(((f32[2048,1024]{1,0:T(8,128)}), f32[512,1024]{1,0:T(8,128)}) %reduce-scatter.19.cloned.1.call-update) | async-done | bytes 2097168 | tf_op jit(solution)/shard_map/reduce_scatter | solution.py:292
  1403.9 79.7 %all-gather.20.cloned.1.call-done = bf16[2048,1024]{1,0:T(8,128)(2,1)} async-done(((bf16[512,1024]{1,0:T(8,128)(2,1)}), bf16[2048,1024]{1,0:T(8,128)(2,1)}) %all-gather.20.cloned.1.call-update) | async-done | bytes 4194320 | tf_op jit(solution)/shard_map/all_gather | solution.py:300
  1483.6 10.6 multiply_reduce_fusion.9
  1503.4 1110.1 %while.42 = (s32[]{:T(128)}, f32[2,128,256]{2,1,0:T(8,128)}, f32[32,64,2,128]{3,1,0,2:T(8,128)}, f32[32,64,2,128]{3,1,0,2:T(8,128)S(1)}, f32[32,64,2,256]{3,1,0,...) while((s32[]{:T(128)}, f32[2,128,256]{2,1,0:T(8,128)}, ...), condition=%wide.region_29.31_spmd.clone, body=%wide.region_19.30_spmd.clone.sunk | while | flops 612151424 | bytes 10787363 | solution.py:161
  2627.9 16.1 multiply_reduce_fusion.8
  2655.6 13.7 multiply_add_fusion
  2683.8 10.7 convolution_convert_fusion
  2706.4 13.3 fusion.156
  2719.9 10.6 fusion.167
  2730.6 12.0 fusion.151
  2743.3 14.6 reduce-scatter.21.cloned.1.call-done
  2760.1 77.5 %reduce-scatter.17.cloned.1.call-done = bf16[512,1024]{1,0:T(8,128)(2,1)} async-done(((bf16[2048,1024]{1,0:T(8,128)(2,1)}), bf16[512,1024]{1,0:T(8,128)(2,1)}) %reduce-scatter.17.cloned.1.call-update) | async-done | bytes 1048592 | tf_op jit(solution)/shard_map/reduce_scatter | solution.py:276
  2850.7 12.6 all-to-all-done.3
  2877.3 37.2 %reduce-scatter.31.cloned.1.call-done = f32[128,4]{1,0:T(8,128)} async-done(((f32[1024,4]{1,0:T(8,128)}), f32[128,4]{1,0:T(8,128)}) %reduce-scatter.31.cloned.1.call-update) | async-done | bytes 2064
  2916.0 42.9 %reduce-scatter.25.cloned.1.call-done = f32[128,2,256]{2,0,1:T(8,128)} async-done(((f32[1024,2,256]{2,0,1:T(8,128)}), f32[128,2,256]{2,0,1:T(8,128)}) %reduce-scatter.25.cloned.1.call-update) | async-done | bytes 262160 | tf_op jit(solution)/shard_map/reduce_scatter | solution.py:331
  2960.7 39.9 %all-reduce.23 = (f32[1024]{0:T(1024)}, f32[1024]{0:T(1024)}, f32[256]{0:T(256)}, f32[8]{0:T(128)}, f32[8]{0:T(128)}) all-reduce(f32[1024]{0:T(1024)S(1)} %get-tuple-element.900, f32[1024]{0:T(1024)S(1)} %copy-done.62, f32[256]{0:T(256)S(1)} %copy-done.78, ...), channel_id=1, replica_groups=mesh['dp'=8,'tensor'=4] {'dp','tensor'}, use_global_device_ids=true, to_apply=%region_45.47 | all-reduce | flops 2320 | bytes 18560 | tf_op jit(solution)/shard_map/psum | solution.py:342
  3006.1 18.7 reduce-scatter.23.cloned.1.call-done
  3027.5 46.1 %reduce-scatter.29.cloned.1.call-done = f32[128,704]{0,1:T(8,128)} async-done(((f32[1024,704]{0,1:T(8,128)}), f32[128,704]{0,1:T(8,128)}) %reduce-scatter.29.cloned.1.call-update) | async-done | bytes 360464 | tf_op jit(solution)/shard_map/reduce_scatter | solution.py:333
  3073.5 63.3 %reduce-scatter.27.cloned.1.call-done = f32[128,2,704]{0,2,1:T(8,128)} async-done(((f32[1024,2,704]{0,2,1:T(8,128)}), f32[128,2,704]{0,2,1:T(8,128)}) %reduce-scatter.27.cloned.1.call-update) | async-done | bytes 720912 | tf_op jit(solution)/shard_map/reduce_scatter | solution.py:332
  (2950 shorter events, 1973.9 us)
Async XLA Ops:
  7.2 61.4 %all-gather.10.cloned.1.call-start = ((), (), s32[]{:S(2)}) async-start(), calls=%async_computation.15 | async-start | bytes 3538944 | tf_op jit(solution)/shard_map/all_gather | solution.py:215
  16.5 23.3 all-to-all-start
  21.7 115.5 %all-gather.8.cloned.1.call-start = ((), (), s32[]{:S(2)}) async-start(), calls=%async_computation.14 | async-start | bytes 5242880 | tf_op jit(solution)/shard_map/all_gather | solution.py:230
  43.6 803.7 %all-gather.12.cloned.1.call-start = ((), (), s32[]{:S(2)}) async-start(), calls=%async_computation.16 | async-start | bytes 1179648 | tf_op jit(solution)/shard_map/all_gather | solution.py:218
  44.4 953.5 %reduce-scatter.15.cloned.1.call-start = ((), (), s32[]{:S(2)}) async-start(), calls=%async_computation.17 | async-start | bytes 10485760 | tf_op jit(solution)/shard_map/reduce_scatter | solution.py:257
  45.1 139.7 %copy-start.70 = (f32[2]{0:T(128)}, f32[2]{0:T(128)S(1)}, u32[]{:S(2)}) copy-start(f32[2]{0:T(128)S(1)} %dynamic_slice.129) | copy-start | bytes 28
  68.6 1333.3 %copy-start.48 = (pred[2048]{0:T(1024)(128)(4,1)}, pred[2048]{0:T(1024)(128)(4,1)S(1)}, u32[]{:S(2)}) copy-start(pred[2048]{0:T(1024)(128)(4,1)S(1)} %get-tuple-element.1016) | copy-start | bytes 6148
  68.6 1334.0 %copy-start.50 = (pred[2048]{0:T(1024)(128)(4,1)}, pred[2048]{0:T(1024)(128)(4,1)S(1)}, u32[]{:S(2)}) copy-start(pred[2048]{0:T(1024)(128)(4,1)S(1)} %get-tuple-element.1017) | copy-start | bytes 6148
  68.6 1334.6 %copy-start.52 = (pred[2048]{0:T(1024)(128)(4,1)}, pred[2048]{0:T(1024)(128)(4,1)S(1)}, u32[]{:S(2)}) copy-start(pred[2048]{0:T(1024)(128)(4,1)S(1)} %get-tuple-element.1018) | copy-start | bytes 6148
  68.6 1415.0 %copy-start.54 = (f32[2048]{0:T(1024)}, f32[2048]{0:T(1024)S(1)}, u32[]{:S(2)}) copy-start(f32[2048]{0:T(1024)S(1)} %get-tuple-element.1015) | copy-start | bytes 24580
  854.8 145.2 %copy-start.32 = (f32[1024]{0:T(1024)S(1)}, f32[1024]{0:T(1024)}, u32[]{:S(2)}) copy-start(f32[1024]{0:T(1024)} %param.34) | copy-start | bytes 12292
  854.8 363.4 %all-gather.16.cloned.1.call-start = ((), (), s32[]{:S(2)}) async-start(), calls=%async_computation.19 | async-start | bytes 3244032 | tf_op jit(solution)/shard_map/all_gather | solution.py:219
  856.7 144.8 %copy-start.4 = (bf16[512,1024]{1,0:T(8,128)(2,1)S(1)}, bf16[512,1024]{1,0:T(8,128)(2,1)}, u32[]{:S(2)}) copy-start(bf16[512,1024]{1,0:T(8,128)(2,1)} %param.23) | copy-start | bytes 3145732
  856.7 361.6 %all-gather.14.cloned.1.call-start = ((), (), s32[]{:S(2)}) async-start(), calls=%async_computation.18 | async-start | bytes 5242880 | tf_op jit(solution)/shard_map/all_gather | solution.py:264
  1000.0 399.6 %copy-start.5 = (f32[512,1024]{1,0:T(8,128)}, f32[512,1024]{1,0:T(8,128)S(1)}, u32[]{:S(2)}) copy-start(f32[512,1024]{1,0:T(8,128)S(1)} %get-tuple-element.970) | copy-start | bytes 6291460
  1000.1 399.6 %copy-start.35 = (f32[512]{0:T(512)}, f32[512]{0:T(512)S(1)}, u32[]{:S(2)}) copy-start(f32[512]{0:T(512)S(1)} %fusion.205) | copy-start | bytes 6148
  1001.5 228.7 %all-gather.18.cloned.1.call-start = ((), (), s32[]{:S(2)}) async-start(), calls=%async_computation.20 | async-start | bytes 1622016 | tf_op jit(solution)/shard_map/all_gather | solution.py:220
  1029.8 25.1 collective-permute-start
  1059.2 153.2 %collective-permute-start.1 = (bf16[2,512,1024]{2,1,0:T(8,128)(2,1)}, bf16[2,512,1024]{2,1,0:T(8,128)(2,1)}, u32[]{:S(2)}, u32[]{:S(2)}) collective-permute-start(bf16[2,512,1024]{2,1,0:T(8,128)(2,1)} %get-tuple-element.1007), channel_id=1, source_target_pairs={{0,2},{1,3},{2,0},{3,1},{4,6},{5,7},{6,4},{7,5},{8,10},{9,11},{10,... | collective-permute-start | bytes 6291464 | tf_op jit(solution)/shard_map/ppermute | solution.py:28
  1062.4 334.4 %reduce-scatter.19.cloned.1.call-start = ((), (), s32[]{:S(2)}) async-start(), calls=%async_computation.22 | async-start | bytes 10485760 | tf_op jit(solution)/shard_map/reduce_scatter | solution.py:292
  1253.3 146.9 %copy-start.13 = (bf16[512,1024]{1,0:T(8,128)(2,1)S(1)}, bf16[512,1024]{1,0:T(8,128)(2,1)}, u32[]{:S(2)}) copy-start(bf16[512,1024]{1,0:T(8,128)(2,1)} %gather_fusion.5) | copy-start | bytes 3145732
  1253.3 230.2 %all-gather.20.cloned.1.call-start = ((), (), s32[]{:S(2)}) async-start(), calls=%async_computation.23 | async-start | bytes 5242880 | tf_op jit(solution)/shard_map/all_gather | solution.py:300
  1401.9 1356.0 %reduce-scatter.21.cloned.1.call-start = ((), (), s32[]{:S(2)}) async-start(), calls=%async_computation.24 | async-start | bytes 5242880 | tf_op jit(solution)/shard_map/reduce_scatter | solution.py:316
  2682.5 155.2 %reduce-scatter.17.cloned.1.call-start = ((), (), s32[]{:S(2)}) async-start(), calls=%async_computation.21 | async-start | bytes 5242880 | tf_op jit(solution)/shard_map/reduce_scatter | solution.py:276
  2694.6 181.1 %reduce-scatter.33.cloned.1.call-start = ((), (), s32[]{:S(2)}) async-start(), calls=%async_computation.30 | async-start | bytes 294912
  2696.3 218.2 %reduce-scatter.31.cloned.1.call-start = ((), (), s32[]{:S(2)}) async-start(), calls=%async_computation.29 | async-start | bytes 589824
  2700.2 258.6 %reduce-scatter.25.cloned.1.call-start = ((), (), s32[]{:S(2)}) async-start(), calls=%async_computation.26 | async-start | bytes 2359296 | tf_op jit(solution)/shard_map/reduce_scatter | solution.py:331
  2706.3 318.5 %reduce-scatter.23.cloned.1.call-start = ((), (), s32[]{:S(2)}) async-start(), calls=%async_computation.25 | async-start | bytes 7077888 | tf_op jit(solution)/shard_map/reduce_scatter | solution.py:328
  2719.7 353.9 %reduce-scatter.29.cloned.1.call-start = ((), (), s32[]{:S(2)}) async-start(), calls=%async_computation.28 | async-start | bytes 3244032 | tf_op jit(solution)/shard_map/reduce_scatter | solution.py:333
  2730.5 406.3 %reduce-scatter.27.cloned.1.call-start = ((), (), s32[]{:S(2)}) async-start(), calls=%async_computation.27 | async-start | bytes 6488064 | tf_op jit(solution)/shard_map/reduce_scatter | solution.py:332
  2844.2 19.1 all-to-all-start.3
  2863.3 140.1 %all-to-all-start.1 = ((bf16[8,64,1024]{2,1,0:T(8,128)(2,1)}), bf16[8,64,1024]{2,1,0:T(8,128)(2,1)S(1)}, u32[]{:S(2)}, u32[]{:S(2)}) async-start(bf16[8,64,1024]{2,1,0:T(8,128)(2,1)} %bitcast.575), calls=%async_computation.3 | async-start | bytes 2097152 | tf_op jit(solution)/shard_map/all_to_all | solution.py:346
  (111 other events, 1889.4 us)
Sparse Core Ops, SparseCore 0:
  10.5 43.6 all-gather.9
  56.4 80.7 all-gather.7
  139.7 22.0 all-gather.11
  854.9 142.8 reduce-scatter.14
  1000.1 40.2 all-gather.15
  1042.5 157.1 all-gather.13
  1202.1 23.1 all-gather.17
  1253.4 143.2 reduce-scatter.18
  1402.0 81.5 all-gather.19
  2682.6 75.2 reduce-scatter.20
  2760.3 77.2 reduce-scatter.16
  2841.1 34.5 reduce-scatter.32
  2879.6 34.7 reduce-scatter.30
  2917.6 41.1 reduce-scatter.24
  2962.4 62.3 reduce-scatter.22
  3028.6 44.8 reduce-scatter.28
  3077.8 58.9 reduce-scatter.26
